TPU v7x, 32 devices: a whole 2x2x4 slice. The times are simulated.
32 devices in a mesh: segment: 4 (over y, x), dom: 8 (over z, core).
Axes of the slice: x: 2, y: 2, z: 4, core: 2. Of those that a mesh axis runs over, the one named last changes fastest.
Arguments:
- features: bfloat16 [4, 4096, 512], P(None, 'dom'), may hold values from -6 to 6
- send_rows: int32 [4, 8, 8, 128], P(None, 'dom'), may hold values from 0 to 511
- send_len: int32 [4, 8, 8], P(None, 'dom'), may hold values from 0 to 128, as said below
- tile_src: int32 [4, 32, 4], P(None, 'dom'), may hold values from 0 to 11
- tile_count: int32 [4, 32], P(None, 'dom'), may hold values from 1 to 4, as said below
- tile_val: bfloat16 [4, 32, 4, 128, 128], P(None, 'dom'), may hold values from -0.25 to 0.25
- w_self: bfloat16 [4, 512, 512], P('segment'), may hold values from -0.25 to 0.25
- w_neigh: bfloat16 [4, 512, 512], P('segment'), may hold values from -0.25 to 0.25
- gain: bfloat16 [4, 512], P('segment'), may hold values from 0.25 to 1.75
- bias: bfloat16 [4, 512], P('segment'), may hold values from -3 to 3
Outputs:
- acts: bfloat16 [4, 4, 4096, 512], P('segment', None, 'dom')
Inputs may be any that keep to these rules, and one draw needn't show every extreme that they name: `send_len`: A partition sends nothing to itself; in every span each partition sends a full block of 128 rows to one other partition. `tile_count`: in every span one partition has 4 live tiles in each of its blocks.
All inputs are finite; a program needn't handle non-finite values.
Results may differ from a plain program's by a relative error of at most 0.0065.
Values may be sent and summed in bfloat16 or wider, within the bound.
No kernel may reach another device: no remote copies, remote signals or barrier semaphores. Data moves between devices by JAX's collectives and lax.ppermute only.
A program may use at most 64 MiB of HBM per device.

v0:
```python
import jax
import jax.numpy as jnp
from jax import lax
from jax.sharding import PartitionSpec as P

norm_eps = 1e-05


def select_span(array_in, span_id):
    return lax.dynamic_index_in_dim(array_in, span_id, 0, keepdims=False)


def sage_layer(inputs, span_id, graph, w_one, w_two, gain_one, bias_one):
    rows_all, lens_all, src_all, count_all, vals_all = graph
    send_list = select_span(rows_all, span_id)[0]
    send_count = select_span(lens_all, span_id)[0]
    tile_index = select_span(src_all, span_id)
    tile_total = select_span(count_all, span_id)
    tile_vals = select_span(vals_all, span_id)
    peer_count, tile_rows = send_list.shape
    feat_width = inputs.shape[1]
    block_count, tile_depth = tile_index.shape
    picked = jnp.take(inputs, send_list.reshape(-1), axis=0).reshape(
        peer_count, tile_rows, feat_width
    )
    row_live = lax.broadcasted_iota(jnp.int32, (peer_count, tile_rows), 1) < send_count[:, None]
    outgoing = jnp.where(row_live[:, :, None], picked, jnp.zeros_like(picked))
    incoming = lax.all_to_all(outgoing, "dom", split_axis=0, concat_axis=0, tiled=True)
    sources = jnp.concatenate(
        [inputs.reshape(block_count, tile_rows, feat_width), incoming], axis=0
    )
    tile_live = lax.broadcasted_iota(jnp.int32, (block_count, tile_depth), 1) < tile_total[:, None]

    def block_sum(packed):
        block_index, block_vals, block_live = packed
        chosen = jnp.take(sources, block_index, axis=0)
        masked = jnp.where(block_live[:, None, None], block_vals, jnp.zeros_like(block_vals))
        return jnp.einsum("kij,kjd->id", masked, chosen, preferred_element_type=jnp.float32)

    summed = lax.map(block_sum, (tile_index, tile_vals, tile_live))
    gathered = summed.reshape(block_count * tile_rows, feat_width).astype(jnp.bfloat16)
    mixed = jnp.dot(inputs, w_one, preferred_element_type=jnp.float32) + jnp.dot(
        gathered, w_two, preferred_element_type=jnp.float32
    )
    center = mixed - jnp.mean(mixed, axis=1, keepdims=True)
    spread = jnp.mean(center * center, axis=1, keepdims=True)
    scaled = center * lax.rsqrt(spread + norm_eps) * gain_one.astype(jnp.float32) + bias_one.astype(
        jnp.float32
    )
    return jnp.maximum(scaled, 0.0).astype(jnp.bfloat16)


def per_device(
    features, send_rows, send_len, tile_src, tile_count, tile_val, w_self, w_neigh, gain, bias
):
    segments = lax.axis_size("segment")
    segment_id = lax.axis_index("segment")
    span_total, node_rows, feat_width = features.shape
    graph = (send_rows, send_len, tile_src, tile_count, tile_val)
    every_self, every_neigh, every_gain, every_bias = (
        lax.all_gather(w_self, "segment", axis=0, tiled=True),
        lax.all_gather(w_neigh, "segment", axis=0, tiled=True),
        lax.all_gather(gain, "segment", axis=0, tiled=True),
        lax.all_gather(bias, "segment", axis=0, tiled=True),
    )
    span_group = span_total // segments
    layers = every_self.shape[0]
    span_id = segment_id * span_group + 0
    hidden = select_span(features, span_id)
    outputs = []
    for layer_id in range(layers):
        hidden = sage_layer(
            hidden,
            span_id,
            graph,
            every_self[layer_id],
            every_neigh[layer_id],
            every_gain[layer_id],
            every_bias[layer_id],
        )
        outputs.append(hidden)
    finished = [jnp.stack(outputs)]
    dealt_out = jnp.stack(finished, axis=1)
    return lax.all_to_all(dealt_out, "segment", split_axis=0, concat_axis=1, tiled=True)


def solution(mesh):
    in_specs = (
        P(None, "dom", None),
        P(None, "dom", None, None),
        P(None, "dom", None),
        P(None, "dom", None),
        P(None, "dom"),
        P(None, "dom", None, None, None),
        P("segment", None, None),
        P("segment", None, None),
        P("segment", None),
        P("segment", None),
    )
    out_specs = P("segment", None, "dom", None)
    return jax.shard_map(
        per_device, mesh=mesh, in_specs=in_specs, out_specs=out_specs, check_vma=False
    )
```

profile of v0, /device:TPU:0, one launch (start us, length us, event | category | flops | bytes accessed | tf_op | source)
XLA Modules:
  0.0 296.5 jit_solution(8535459585677246511)
XLA Ops:
  8.2 5.1 %gather_fusion.4 = bf16[1024,512]{1,0:T(8,128)(2,1)} fusion(bf16[512,512]{1,0:T(8,128)(2,1)S(1)} %fusion.67, s32[1024]{0:T(1024)S(1)} %fusion.49), kind=kCustom, calls=%fused_computation.clone | custom fusion | bytes 2101248 | tf_op jit(solution)/shard_map/jit(_take)/gather | solution.py:23
  17.3 6.5 %all-to-all-start = ((bf16[8,128,512]{2,1,0:T(8,128)(2,1)}), bf16[8,128,512]{2,1,0:T(8,128)(2,1)}, u32[]{:S(2)}, u32[]{:S(2)}) async-start(bf16[8,128,512]{2,1,0:T(8,128)(2,1)} %broadcast_select_fusion.7), calls=%async_computation | async-start | bytes 2097152 | tf_op jit(solution)/shard_map/all_to_all | solution.py:28
  24.5 8.1 %all-gather = bf16[4,1,512]{2,1,0:T(2,128)(2,1)S(1)} all-gather(bf16[1,1,512]{2,1,0:T(2,128)(2,1)S(1)} %bitcast.203), channel_id=1, replica_groups=mesh['segment'=4,'dom'=8] {'segment'}, dimensions={0}, use_global_device_ids=true | all-gather | bytes 5120 | tf_op jit(solution)/shard_map/all_gather | solution.py:63
  34.1 8.3 %all-gather.1 = bf16[4,1,512]{2,1,0:T(2,128)(2,1)S(1)} all-gather(bf16[1,1,512]{2,1,0:T(2,128)(2,1)S(1)} %bitcast.204), channel_id=1, replica_groups=mesh['segment'=4,'dom'=8] {'segment'}, dimensions={0}, use_global_device_ids=true | all-gather | bytes 5120 | tf_op jit(solution)/shard_map/all_gather | solution.py:64
  42.4 1.9 dynamic-slice_bitcast_fusion.4
  44.3 6.1 %all-to-all-done = bf16[8,128,512]{2,1,0:T(8,128)(2,1)} async-done(((bf16[8,128,512]{2,1,0:T(8,128)(2,1)}), bf16[8,128,512]{2,1,0:T(8,128)(2,1)}, u32[]{:S(2)}, u32[]{:S(2)}) %all-to-all-start) | async-done | bytes 1048608 | tf_op jit(solution)/shard_map/all_to_all | solution.py:28
  50.4 2.5 pad_maximum_fusion
  53.8 15.7 %while.40 = (s32[]{:T(128)}, bf16[4,128,512]{2,1,0:T(8,128)(2,1)}, pred[4,4]{1,0:T(4,128)(4,1)S(1)}, bf16[4,4,128,128]{3,2,1,0:T(8,128)(2,1)}, s32[4,4]{1,0:T(4,...) while((s32[]{:T(128)}, bf16[4,128,512]{2,1,0:T(8,128)(2,1)}, pred[4,4]{1,0:T(4,128)(4,1)S(1)}, ...), condition=%wide.region_1.4_spmd, body=%wide.region_0.3_spmd.sunk | while | flops 67437592 | bytes 1971369 | solution.py:40
  53.8 2.0 gather_fusion
  57.8 2.0 gather_fusion
  61.7 2.0 gather_fusion
  65.6 2.0 gather_fusion
  69.5 2.5 fusion.48
  72.0 12.2 %all-gather.7.cloned.1.call-done = bf16[4,512,512]{2,1,0:T(8,128)(2,1)} async-done(((bf16[1,512,512]{2,1,0:T(8,128)(2,1)}), bf16[4,512,512]{2,1,0:T(8,128)(2,1)}) %all-gather.7.cloned.1.call-update) | async-done | bytes 2097168 | tf_op jit(solution)/shard_map/all_gather | solution.py:62
  87.4 5.1 %gather_fusion.5 = bf16[1024,512]{1,0:T(8,128)(2,1)} fusion(bf16[512,512]{1,0:T(8,128)(2,1)S(1)} %maximum_convert_fusion.3, s32[1024]{0:T(1024)S(1)} %fusion.49), kind=kCustom, calls=%fused_computation.2.clone | custom fusion | bytes 2101248 | tf_op jit(solution)/shard_map/jit(_take)/gather | solution.py:23
  95.1 4.6 %all-to-all-start.1 = ((bf16[8,128,512]{2,1,0:T(8,128)(2,1)}), bf16[8,128,512]{2,1,0:T(8,128)(2,1)}, u32[]{:S(2)}, u32[]{:S(2)}) async-start(bf16[8,128,512]{2,1,0:T(8,128)(2,1)} %broadcast_select_fusion.6), calls=%async_computation.1 | async-start | bytes 2097152 | tf_op jit(solution)/shard_map/all_to_all | solution.py:28
  99.7 2.5 fusion.47
  102.2 24.2 %all-to-all-done.1 = bf16[8,128,512]{2,1,0:T(8,128)(2,1)} async-done(((bf16[8,128,512]{2,1,0:T(8,128)(2,1)}), bf16[8,128,512]{2,1,0:T(8,128)(2,1)}, u32[]{:S(2)}, u32[]{:S(2)}) %all-to-all-start.1) | async-done | bytes 1048608 | tf_op jit(solution)/shard_map/all_to_all | solution.py:28
  126.4 2.5 pad_maximum_fusion.1
  128.9 13.2 %while.41 = (s32[]{:T(128)}, bf16[4,128,512]{2,1,0:T(8,128)(2,1)S(1)}, pred[4,4]{1,0:T(4,128)(4,1)S(1)}, bf16[4,4,128,128]{3,2,1,0:T(8,128)(2,1)}, s32[4,4]{1,0:...) while((s32[]{:T(128)}, bf16[4,128,512]{2,1,0:T(8,128)(2,1)S(1)}, pred[4,4]{1,0:T(4,128)(4,1)S(1)}, ...), condition=%wide.region_5.8_spmd, body=%wide.region_4.7_spmd.sunk | while | flops 67437592 | bytes 1972385 | solution.py:40
  129.0 2.0 gather_fusion.1
  132.2 2.0 gather_fusion.1
  135.5 2.0 gather_fusion.1
  138.8 2.0 gather_fusion.1
  142.1 1.9 fusion.54
  145.3 5.1 %gather_fusion.6 = bf16[1024,512]{1,0:T(8,128)(2,1)} fusion(bf16[512,512]{1,0:T(8,128)(2,1)S(1)} %maximum_convert_fusion.2, s32[1024]{0:T(1024)S(1)} %fusion.49), kind=kCustom, calls=%fused_computation.3.clone | custom fusion | bytes 2101248 | tf_op jit(solution)/shard_map/jit(_take)/gather | solution.py:23
  153.0 4.3 %all-to-all-start.2 = ((bf16[8,128,512]{2,1,0:T(8,128)(2,1)}), bf16[8,128,512]{2,1,0:T(8,128)(2,1)}, u32[]{:S(2)}, u32[]{:S(2)}) async-start(bf16[8,128,512]{2,1,0:T(8,128)(2,1)} %broadcast_select_fusion.5), calls=%async_computation.2 | async-start | bytes 2097152 | tf_op jit(solution)/shard_map/all_to_all | solution.py:28
  157.2 2.5 fusion.46
  159.7 24.1 %all-to-all-done.2 = bf16[8,128,512]{2,1,0:T(8,128)(2,1)} async-done(((bf16[8,128,512]{2,1,0:T(8,128)(2,1)}), bf16[8,128,512]{2,1,0:T(8,128)(2,1)}, u32[]{:S(2)}, u32[]{:S(2)}) %all-to-all-start.2) | async-done | bytes 1048608 | tf_op jit(solution)/shard_map/all_to_all | solution.py:28
  183.8 2.5 pad_maximum_fusion.2
  186.3 13.2 %while.42 = (s32[]{:T(128)}, bf16[4,128,512]{2,1,0:T(8,128)(2,1)S(1)}, pred[4,4]{1,0:T(4,128)(4,1)S(1)}, bf16[4,4,128,128]{3,2,1,0:T(8,128)(2,1)}, s32[4,4]{1,0:...) while((s32[]{:T(128)}, bf16[4,128,512]{2,1,0:T(8,128)(2,1)S(1)}, pred[4,4]{1,0:T(4,128)(4,1)S(1)}, ...), condition=%wide.region_9.12_spmd, body=%wide.region_8.11_spmd.sunk | while | flops 67437592 | bytes 1972385 | solution.py:40
  186.4 2.0 gather_fusion.2
  189.7 2.0 gather_fusion.2
  193.0 2.0 gather_fusion.2
  196.2 2.0 gather_fusion.2
  202.7 5.1 %gather_fusion.7 = bf16[1024,512]{1,0:T(8,128)(2,1)} fusion(bf16[512,512]{1,0:T(8,128)(2,1)S(1)} %maximum_convert_fusion.1, s32[1024]{0:T(1024)S(1)} %fusion.49), kind=kCustom, calls=%fused_computation.4.clone | custom fusion | bytes 2101248 | tf_op jit(solution)/shard_map/jit(_take)/gather | solution.py:23
  210.4 4.2 %all-to-all-start.3 = ((bf16[8,128,512]{2,1,0:T(8,128)(2,1)}), bf16[8,128,512]{2,1,0:T(8,128)(2,1)}, u32[]{:S(2)}, u32[]{:S(2)}) async-start(bf16[8,128,512]{2,1,0:T(8,128)(2,1)} %broadcast_select_fusion.4), calls=%async_computation.3 | async-start | bytes 2097152 | tf_op jit(solution)/shard_map/all_to_all | solution.py:28
  214.7 2.5 fusion.64
  219.3 2.5 fusion.45
  221.8 19.4 %all-to-all-done.3 = bf16[8,128,512]{2,1,0:T(8,128)(2,1)} async-done(((bf16[8,128,512]{2,1,0:T(8,128)(2,1)}), bf16[8,128,512]{2,1,0:T(8,128)(2,1)}, u32[]{:S(2)}, u32[]{:S(2)}) %all-to-all-start.3) | async-done | bytes 1048608 | tf_op jit(solution)/shard_map/all_to_all | solution.py:28
  241.2 2.5 pad_maximum_fusion.3
  243.8 13.2 %while.43 = (s32[]{:T(128)}, bf16[4,128,512]{2,1,0:T(8,128)(2,1)S(1)}, pred[4,4]{1,0:T(4,128)(4,1)S(1)}, bf16[4,4,128,128]{3,2,1,0:T(8,128)(2,1)}, s32[4,4]{1,0:...) while((s32[]{:T(128)}, bf16[4,128,512]{2,1,0:T(8,128)(2,1)S(1)}, pred[4,4]{1,0:T(4,128)(4,1)S(1)}, ...), condition=%wide.region_13.16_spmd, body=%wide.region_12.15_spmd.sunk | while | flops 67437592 | bytes 1972385 | solution.py:40
  243.8 2.0 gather_fusion.3
  247.1 2.0 gather_fusion.3
  250.4 2.0 gather_fusion.3
  253.7 2.0 gather_fusion.3
  256.9 1.9 fusion.56
  260.5 27.8 %all_to_all.32 = bf16[4,1,512,512]{3,2,1,0:T(8,128)(2,1)S(1)} all-to-all(bf16[4,1,512,512]{3,2,1,0:T(8,128)(2,1)S(1)} %maximum_bitcast_fusion), channel_id=1, replica_groups=mesh['segment'=4,'dom'=8] {'segment'}, dimensions={0} | all-to-all | bytes 4194304 | tf_op jit(solution)/shard_map/all_to_all | solution.py:84
  (138 shorter events, 52.0 us)
Async XLA Ops:
  6.5 1.6 copy-start
  6.5 63.0 %all-gather.5.cloned.1.call-start = ((), (), s32[]{:S(2)}) async-start(), calls=%async_computation.5 | async-start | bytes 2621440 | tf_op jit(solution)/shard_map/all_gather | solution.py:61
  16.1 8.4 %copy-start.10 = (bf16[1,512]{1,0:T(2,128)(2,1)S(1)}, bf16[1,512]{1,0:T(2,128)(2,1)}, u32[]{:S(2)}) copy-start(bf16[1,512]{1,0:T(2,128)(2,1)} %param.30) | copy-start | bytes 3076
  17.3 16.9 %copy-start.11 = (bf16[1,512]{1,0:T(2,128)(2,1)S(1)}, bf16[1,512]{1,0:T(2,128)(2,1)}, u32[]{:S(2)}) copy-start(bf16[1,512]{1,0:T(2,128)(2,1)} %param.31) | copy-start | bytes 3076
  17.3 33.2 %all-to-all-start = ((bf16[8,128,512]{2,1,0:T(8,128)(2,1)}), bf16[8,128,512]{2,1,0:T(8,128)(2,1)}, u32[]{:S(2)}, u32[]{:S(2)}) async-start(bf16[8,128,512]{2,1,0:T(8,128)(2,1)} %broadcast_select_fusion.7), calls=%async_computation | async-start | bytes 2097152 | tf_op jit(solution)/shard_map/all_to_all | solution.py:28
  23.8 60.4 %all-gather.7.cloned.1.call-start = ((), (), s32[]{:S(2)}) async-start(), calls=%async_computation.6 | async-start | bytes 2621440 | tf_op jit(solution)/shard_map/all_gather | solution.py:62
  69.5 14.7 %copy-start.6 = (bf16[4,128,512]{2,1,0:T(8,128)(2,1)S(1)}, bf16[4,128,512]{2,1,0:T(8,128)(2,1)}, u32[]{:S(2)}) copy-start(bf16[4,128,512]{2,1,0:T(8,128)(2,1)} %get-tuple-element.135) | copy-start | bytes 1572868
  86.1 1.0 copy-start.1
  95.1 31.3 %all-to-all-start.1 = ((bf16[8,128,512]{2,1,0:T(8,128)(2,1)}), bf16[8,128,512]{2,1,0:T(8,128)(2,1)}, u32[]{:S(2)}, u32[]{:S(2)}) async-start(bf16[8,128,512]{2,1,0:T(8,128)(2,1)} %broadcast_select_fusion.6), calls=%async_computation.1 | async-start | bytes 2097152 | tf_op jit(solution)/shard_map/all_to_all | solution.py:28
  144.0 1.0 copy-start.2
  153.0 30.8 %all-to-all-start.2 = ((bf16[8,128,512]{2,1,0:T(8,128)(2,1)}), bf16[8,128,512]{2,1,0:T(8,128)(2,1)}, u32[]{:S(2)}, u32[]{:S(2)}) async-start(bf16[8,128,512]{2,1,0:T(8,128)(2,1)} %broadcast_select_fusion.5), calls=%async_computation.2 | async-start | bytes 2097152 | tf_op jit(solution)/shard_map/all_to_all | solution.py:28
  201.4 1.0 copy-start.4
  210.4 30.8 %all-to-all-start.3 = ((bf16[8,128,512]{2,1,0:T(8,128)(2,1)}), bf16[8,128,512]{2,1,0:T(8,128)(2,1)}, u32[]{:S(2)}, u32[]{:S(2)}) async-start(bf16[8,128,512]{2,1,0:T(8,128)(2,1)} %broadcast_select_fusion.4), calls=%async_computation.3 | async-start | bytes 2097152 | tf_op jit(solution)/shard_map/all_to_all | solution.py:28
  214.7 2.5 copy-start.3
  214.7 3.6 %copy-start.5 = (f32[512,512]{1,0:T(8,128)S(1)}, f32[512,512]{1,0:T(8,128)}, u32[]{:S(2)}) copy-start(f32[512,512]{1,0:T(8,128)} %copy-done.4) | copy-start | bytes 3145732
  258.9 1.0 copy-start.7
  258.9 1.2 copy-start.8
  258.9 1.3 copy-start.9
Sparse Core Ops, SparseCore 0:
  9.2 37.9 all-gather.4
  49.0 35.1 all-gather.6
where the time goes:
time: 298 us; the launch traced here: 296 us
  waiting for transfers between devices  87.4 us (29%)
  local copies, waits for them, and re-layouts  61.9 us (21%)
  blocking collectives  44.2 us (15%)
  matrix products  39.7 us (13%)
  other arithmetic  29.3 us (10%)
  starting transfers between devices  19.6 us (7%)
  between operations  13.7 us (5%)
    all_to_all x4, waiting for transfers between devices, sage_layer(): lax.all_to_all(outgoing, 'dom', split_axis=0, concat_axis=0, tiled=True)  73.8 us
    gather x16, local copies, waits for them, and re-layouts, block_sum(): chosen = jnp.take(sources, block_index, axis=0)  31.8 us
    all_to_all x1, blocking collectives, per_device(): lax.all_to_all(dealt_out, 'segment', split_axis=0, concat_axis=1, tiled=T...  27.8 us
    dot_general x16, matrix products, block_sum(): jnp.einsum('kij,kjd->id', masked, chosen, preferred_element_type=jnp.floa...  22.2 us
    gather x4, local copies, waits for them, and re-layouts, sage_layer(): jnp.take(inputs, send_list.reshape(-1), axis=0)  20.3 us
    all_to_all x4, starting transfers between devices, sage_layer(): lax.all_to_all(outgoing, 'dom', split_axis=0, concat_axis=0, tiled=True)  19.6 us
    all_gather x1, waiting for transfers between devices, per_device(): lax.all_gather(w_neigh, 'segment', axis=0, tiled=True)  12.2 us
    concatenate x4, other arithmetic, sage_layer(): jnp.concatenate([inputs.reshape(block_count, tile_rows, feat_width), inco...  10 us
  transfers between devices with their start and end apart: 6, of which 5 were waited for; matrix products, arithmetic and copies ran while one was open for 16% of the time, Pallas kernels for 0%

commit v1 on v0

--- a/solution.py
+++ b/solution.py
@@ -4,6 +4,20 @@
 from jax.sharding import PartitionSpec as P
 
 norm_eps = 1e-05
+
+
+def convert_cells(tile_in, d0, m):
+    everything = tile_in.shape
+    prior = tile_in.reshape(*everything[:d0], m, everything[d0] // m, *everything[d0 + 1 :])
+    return jnp.moveaxis(prior, d0, 0)
+
+
+def supply_all_clusters_by_axis(in_array, ndim_at):
+    in_array = jnp.moveaxis(in_array, 0, ndim_at)
+    clean = in_array.shape
+    return in_array.reshape(
+        *clean[:ndim_at], clean[ndim_at] * clean[ndim_at + 1], *clean[ndim_at + 2 :]
+    )
 
 
 def select_span(array_in, span_id):
@@ -25,7 +39,18 @@
     )
     row_live = lax.broadcasted_iota(jnp.int32, (peer_count, tile_rows), 1) < send_count[:, None]
     outgoing = jnp.where(row_live[:, :, None], picked, jnp.zeros_like(picked))
-    incoming = lax.all_to_all(outgoing, "dom", split_axis=0, concat_axis=0, tiled=True)
+    inter = lax.axis_size("dom")
+    next_value, frame_out = (inter, lax.axis_index("dom"))
+    oldest = convert_cells(outgoing, 0, next_value)
+    found = [oldest[frame_out]]
+    for num in range(1, next_value):
+        part_next = oldest[frame_out ^ num]
+        all_rows = lax.ppermute(
+            part_next, axis_name="dom", perm=[(rr, rr ^ num) for rr in range(next_value)]
+        )
+        found.append(all_rows)
+    oldest = jnp.stack(found)[frame_out ^ jnp.arange(next_value)]
+    incoming = supply_all_clusters_by_axis(oldest, 0)
     sources = jnp.concatenate(
         [inputs.reshape(block_count, tile_rows, feat_width), incoming], axis=0
     )

time: 298 us -> 273 us (0.916)
  waiting for transfers between devices: 87.4 us -> 61.6 us
  starting transfers between devices: 19.6 us -> 41.7 us
  other arithmetic: 29.3 us -> 13.9 us
  local copies, waits for them, and re-layouts: 61.9 us -> 47.5 us
  matrix products: 39.7 us -> 44.2 us
    all_to_all x4 -> x0, waiting for transfers between devices: 73.8 us -> none  [sage_layer(): lax.all_to_all(outgoing, 'dom', split_axis=0, concat_axis=0, tiled=True)]
    ppermute x0 -> x28, waiting for transfers between devices: none -> 46.6 us  [sage_layer(): lax.ppermute(part_next, axis_name='dom', perm=[(rr, rr ^ num) for rr in r...]
    ppermute x0 -> x28, starting transfers between devices: none -> 41.7 us  [sage_layer(): lax.ppermute(part_next, axis_name='dom', perm=[(rr, rr ^ num) for rr in r...]
    gather x16, local copies, waits for them, and re-layouts: 31.8 us -> 9.29 us  [block_sum(): chosen = jnp.take(sources, block_index, axis=0)]
    all_to_all x4 -> x0, starting transfers between devices: 19.6 us -> none  [sage_layer(): lax.all_to_all(outgoing, 'dom', split_axis=0, concat_axis=0, tiled=True)]
    concatenate x4, other arithmetic: 10 us -> 1.78 us  [sage_layer(): jnp.concatenate([inputs.reshape(block_count, tile_rows, feat_width), inco...]
    unnamed x25 -> x71, local copies, waits for them, and re-layouts: 4.51 us -> 10.4 us
    dot_general x16, matrix products: 22.2 us -> 27.3 us  [block_sum(): jnp.einsum('kij,kjd->id', masked, chosen, preferred_element_type=jnp.floa...]
  transfers between devices with their start and end apart: 6 -> 30, of which waited for: 5 -> 10; matrix products, arithmetic and copies ran while one was open for 16% -> 16% of each run, Pallas kernels for 0% -> 0%
where the time goes in v1:
time: 273 us; the launch traced here: 269 us
  waiting for transfers between devices  61.6 us (23%)
  local copies, waits for them, and re-layouts  47.5 us (17%)
  blocking collectives  45.4 us (17%)
  matrix products  44.2 us (16%)
  starting transfers between devices  41.7 us (15%)
  between operations  14.2 us (5%)
  other arithmetic  13.9 us (5%)
    ppermute x28, waiting for transfers between devices, sage_layer(): lax.ppermute(part_next, axis_name='dom', perm=[(rr, rr ^ num) for rr in r...  46.6 us
    ppermute x28, starting transfers between devices, sage_layer(): lax.ppermute(part_next, axis_name='dom', perm=[(rr, rr ^ num) for rr in r...  41.7 us
    all_to_all x1, blocking collectives, per_device(): lax.all_to_all(dealt_out, 'segment', split_axis=0, concat_axis=1, tiled=T...  28.9 us
    dot_general x16, matrix products, block_sum(): jnp.einsum('kij,kjd->id', masked, chosen, preferred_element_type=jnp.floa...  27.3 us
    gather x4, local copies, waits for them, and re-layouts, sage_layer(): jnp.take(inputs, send_list.reshape(-1), axis=0)  17 us
    all_gather x1, waiting for transfers between devices, per_device(): lax.all_gather(w_neigh, 'segment', axis=0, tiled=True)  14.3 us
    unnamed x71, local copies, waits for them, and re-layouts  10.4 us
    dot_general x4, matrix products, sage_layer(): jnp.dot(inputs, w_one, preferred_element_type=jnp.float32)  9.79 us
  transfers between devices with their start and end apart: 30, of which 10 were waited for; matrix products, arithmetic and copies ran while one was open for 16% of the time, Pallas kernels for 0%

profile of v1, /device:TPU:0, one launch (start us, length us, event | category | flops | bytes accessed | tf_op | source)
XLA Modules:
  0.0 269.0 jit_solution(9044457115183121006)
XLA Ops:
  8.2 5.1 %gather_fusion.8 = bf16[1024,512]{1,0:T(8,128)(2,1)} fusion(bf16[512,512]{1,0:T(8,128)(2,1)S(1)} %fusion.70, s32[1024]{0:T(1024)S(1)} %fusion.50), kind=kCustom, calls=%fused_computation.clone | custom fusion | bytes 2101248 | tf_op jit(solution)/shard_map/jit(_take)/gather | solution.py:37
  17.9 2.6 collective-permute-start.1
  20.6 2.8 %collective-permute-start.3 = (bf16[1,128,512]{2,1,0:T(8,128)(2,1)S(1)}, bf16[1,128,512]{2,1,0:T(8,128)(2,1)}, u32[]{:S(2)}, u32[]{:S(2)}) collective-permute-start(bf16[1,128,512]{2,1,0:T(8,128)(2,1)S(1)} %get-tuple-element.219), channel_id=1, source_target_pairs={{0,4},{1,5},{2,6},{3,7},{4,0},{5,1},{6,2},{7,3},{8,12},{9,13},{10,... | collective-permute-start | bytes 393224 | tf_op jit(solution)/shard_map/ppermute | solution.py:48
  25.7 8.1 %all-gather = bf16[4,1,512]{2,1,0:T(2,128)(2,1)S(1)} all-gather(bf16[1,1,512]{2,1,0:T(2,128)(2,1)S(1)} %bitcast.279), channel_id=1, replica_groups=mesh['segment'=4,'dom'=8] {'segment'}, dimensions={0}, use_global_device_ids=true | all-gather | bytes 5120 | tf_op jit(solution)/shard_map/all_gather | solution.py:88
  34.5 8.4 %all-gather.1 = bf16[4,1,512]{2,1,0:T(2,128)(2,1)S(1)} all-gather(bf16[1,1,512]{2,1,0:T(2,128)(2,1)} %bitcast.280), channel_id=1, replica_groups=mesh['segment'=4,'dom'=8] {'segment'}, dimensions={0}, use_global_device_ids=true | all-gather | bytes 5120 | tf_op jit(solution)/shard_map/all_gather | solution.py:89
  44.1 1.9 dynamic-slice_bitcast_fusion.4
  46.0 3.6 %collective-permute-start.5 = (bf16[1,128,512]{2,1,0:T(8,128)(2,1)S(1)}, bf16[1,128,512]{2,1,0:T(8,128)(2,1)S(1)}, u32[]{:S(2)}, u32[]{:S(2)}) collective-permute-start(bf16[1,128,512]{2,1,0:T(8,128)(2,1)S(1)} %get-tuple-element.217), channel_id=1, source_target_pairs={{0,6},{1,7},{2,4},{3,5},{4,2},{5,3},{6,0},{7,1},{8,14},{9,15},{10,... | collective-permute-start | bytes 393224 | tf_op jit(solution)/shard_map/ppermute | solution.py:48
  54.4 2.5 collective-permute-done.6
  59.9 7.5 %while.40 = (s32[]{:T(128)}, bf16[4,128,512]{2,1,0:T(8,128)(2,1)S(1)}, pred[4,4]{1,0:T(4,128)(4,1)S(1)}, bf16[4,4,128,128]{3,2,1,0:T(8,128)(2,1)}, s32[4,4]{1,0:...) while((s32[]{:T(128)}, bf16[4,128,512]{2,1,0:T(8,128)(2,1)S(1)}, pred[4,4]{1,0:T(4,128)(4,1)S(1)}, ...), condition=%wide.region_1.4_spmd, body=%wide.region_0.3_spmd.sunk | while | flops 67437592 | bytes 1972385 | solution.py:65
  67.5 2.4 fusion.48
  69.9 14.3 %all-gather.7.cloned.1.call-done = bf16[4,512,512]{2,1,0:T(8,128)(2,1)} async-done(((bf16[1,512,512]{2,1,0:T(8,128)(2,1)}), bf16[4,512,512]{2,1,0:T(8,128)(2,1)}) %all-gather.7.cloned.1.call-update) | async-done | bytes 2097168 | tf_op jit(solution)/shard_map/all_gather | solution.py:87
  84.2 1.9 fusion.56
  86.7 4.0 %gather_fusion.9 = bf16[1024,512]{1,0:T(8,128)(2,1)S(1)} fusion(bf16[512,512]{1,0:T(8,128)(2,1)S(1)} %maximum_convert_fusion.3, s32[1024]{0:T(1024)S(1)} %fusion.50), kind=kCustom, calls=%fused_computation.2.clone | custom fusion | bytes 2101248 | tf_op jit(solution)/shard_map/jit(_take)/gather | solution.py:37
  91.7 2.4 fusion.47
  97.1 2.4 collective-permute-start.10
  99.7 3.4 %collective-permute-start.12 = (bf16[1,128,512]{2,1,0:T(8,128)(2,1)S(1)}, bf16[1,128,512]{2,1,0:T(8,128)(2,1)S(1)}, u32[]{:S(2)}, u32[]{:S(2)}) collective-permute-start(bf16[1,128,512]{2,1,0:T(8,128)(2,1)S(1)} %get-tuple-element.210), channel_id=1, source_target_pairs={{0,6},{1,7},{2,4},{3,5},{4,2},{5,3},{6,0},{7,1},{8,14},{9,15},{10,... | collective-permute-start | bytes 393224 | tf_op jit(solution)/shard_map/ppermute | solution.py:48
  103.1 3.5 %collective-permute-done.8 = bf16[1,128,512]{2,1,0:T(8,128)(2,1)S(1)} collective-permute-done((bf16[1,128,512]{2,1,0:T(8,128)(2,1)S(1)}, bf16[1,128,512]{2,1,0:T(8,128)(2,1)S(1)}, u32[]{:S(2)}, u32[]{:S(2)}) %collective-permute-start.8) | collective-permute-done | bytes 131104 | tf_op jit(solution)/shard_map/ppermute | solution.py:48
  108.5 8.9 %collective-permute-done.11 = bf16[1,128,512]{2,1,0:T(8,128)(2,1)S(1)} collective-permute-done((bf16[1,128,512]{2,1,0:T(8,128)(2,1)S(1)}, bf16[1,128,512]{2,1,0:T(8,128)(2,1)S(1)}, u32[]{:S(2)}, u32[]{:S(2)}) %collective-permute-start.11) | collective-permute-done | bytes 131104 | tf_op jit(solution)/shard_map/ppermute | solution.py:48
  119.2 10.0 %while.41 = (s32[]{:T(128)}, bf16[4,128,512]{2,1,0:T(8,128)(2,1)}, pred[4,4]{1,0:T(4,128)(4,1)S(1)}, bf16[4,4,128,128]{3,2,1,0:T(8,128)(2,1)}, s32[4,4]{1,0:T(4,...) while((s32[]{:T(128)}, bf16[4,128,512]{2,1,0:T(8,128)(2,1)}, pred[4,4]{1,0:T(4,128)(4,1)S(1)}, ...), condition=%wide.region_5.8_spmd, body=%wide.region_4.7_spmd.sunk | while | flops 67437592 | bytes 1971369 | solution.py:65
  119.9 1.9 fusion.82
  122.4 1.9 fusion.82
  124.9 1.9 fusion.82
  127.4 1.9 fusion.82
  131.6 4.0 %gather_fusion.10 = bf16[1024,512]{1,0:T(8,128)(2,1)S(1)} fusion(bf16[512,512]{1,0:T(8,128)(2,1)S(1)} %maximum_convert_fusion.2, s32[1024]{0:T(1024)S(1)} %fusion.50), kind=kCustom, calls=%fused_computation.3.clone | custom fusion | bytes 2101248 | tf_op jit(solution)/shard_map/jit(_take)/gather | solution.py:37
  136.6 2.4 fusion.46
  140.2 5.9 %collective-permute-start.15 = (bf16[1,128,512]{2,1,0:T(8,128)(2,1)S(1)}, bf16[1,128,512]{2,1,0:T(8,128)(2,1)S(1)}, u32[]{:S(2)}, u32[]{:S(2)}) collective-permute-start(bf16[1,128,512]{2,1,0:T(8,128)(2,1)S(1)} %get-tuple-element.207), channel_id=1, source_target_pairs={{0,2},{1,3},{2,0},{3,1},{4,6},{5,7},{6,4},{7,5},{8,10},{9,11},{10,... | collective-permute-start | bytes 393224 | tf_op jit(solution)/shard_map/ppermute | solution.py:48
  146.2 3.0 %collective-permute-start.17 = (bf16[1,128,512]{2,1,0:T(8,128)(2,1)S(1)}, bf16[1,128,512]{2,1,0:T(8,128)(2,1)S(1)}, u32[]{:S(2)}, u32[]{:S(2)}) collective-permute-start(bf16[1,128,512]{2,1,0:T(8,128)(2,1)S(1)} %get-tuple-element.205), channel_id=1, source_target_pairs={{0,4},{1,5},{2,6},{3,7},{4,0},{5,1},{6,2},{7,3},{8,12},{9,13},{10,... | collective-permute-start | bytes 393224 | tf_op jit(solution)/shard_map/ppermute | solution.py:48
  149.6 2.1 collective-permute-start.19
  153.0 4.6 %collective-permute-done.16 = bf16[1,128,512]{2,1,0:T(8,128)(2,1)S(1)} collective-permute-done((bf16[1,128,512]{2,1,0:T(8,128)(2,1)S(1)}, bf16[1,128,512]{2,1,0:T(8,128)(2,1)S(1)}, u32[]{:S(2)}, u32[]{:S(2)}) %collective-permute-start.16) | collective-permute-done | bytes 131104 | tf_op jit(solution)/shard_map/ppermute | solution.py:48
  157.7 9.7 %collective-permute-done.18 = bf16[1,128,512]{2,1,0:T(8,128)(2,1)S(1)} collective-permute-done((bf16[1,128,512]{2,1,0:T(8,128)(2,1)S(1)}, bf16[1,128,512]{2,1,0:T(8,128)(2,1)S(1)}, u32[]{:S(2)}, u32[]{:S(2)}) %collective-permute-start.18) | collective-permute-done | bytes 131104 | tf_op jit(solution)/shard_map/ppermute | solution.py:48
  169.3 10.0 %while.42 = (s32[]{:T(128)}, bf16[4,128,512]{2,1,0:T(8,128)(2,1)}, pred[4,4]{1,0:T(4,128)(4,1)S(1)}, bf16[4,4,128,128]{3,2,1,0:T(8,128)(2,1)}, s32[4,4]{1,0:T(4,...) while((s32[]{:T(128)}, bf16[4,128,512]{2,1,0:T(8,128)(2,1)}, pred[4,4]{1,0:T(4,128)(4,1)S(1)}, ...), condition=%wide.region_9.12_spmd, body=%wide.region_8.11_spmd.sunk | while | flops 67437592 | bytes 1971369 | solution.py:65
  169.9 1.9 fusion.84
  172.4 1.9 fusion.84
  174.9 1.9 fusion.84
  177.4 1.9 fusion.84
  181.6 4.0 %gather_fusion.11 = bf16[1024,512]{1,0:T(8,128)(2,1)S(1)} fusion(bf16[512,512]{1,0:T(8,128)(2,1)S(1)} %maximum_convert_fusion.1, s32[1024]{0:T(1024)S(1)} %fusion.50), kind=kCustom, calls=%fused_computation.4.clone | custom fusion | bytes 2101248 | tf_op jit(solution)/shard_map/jit(_take)/gather | solution.py:37
  186.3 2.4 fusion.45
  189.8 6.1 %collective-permute-start.22 = (bf16[1,128,512]{2,1,0:T(8,128)(2,1)S(1)}, bf16[1,128,512]{2,1,0:T(8,128)(2,1)S(1)}, u32[]{:S(2)}, u32[]{:S(2)}) collective-permute-start(bf16[1,128,512]{2,1,0:T(8,128)(2,1)S(1)} %get-tuple-element.200), channel_id=1, source_target_pairs={{0,2},{1,3},{2,0},{3,1},{4,6},{5,7},{6,4},{7,5},{8,10},{9,11},{10,... | collective-permute-start | bytes 393224 | tf_op jit(solution)/shard_map/ppermute | solution.py:48
  195.9 1.9 collective-permute-start.24
  198.3 2.1 collective-permute-start.26
  200.4 4.1 %collective-permute-done.22 = bf16[1,128,512]{2,1,0:T(8,128)(2,1)S(1)} collective-permute-done((bf16[1,128,512]{2,1,0:T(8,128)(2,1)S(1)}, bf16[1,128,512]{2,1,0:T(8,128)(2,1)S(1)}, u32[]{:S(2)}, u32[]{:S(2)}) %collective-permute-start.22) | collective-permute-done | bytes 131104 | tf_op jit(solution)/shard_map/ppermute | solution.py:48
  204.5 2.6 collective-permute-done.23
  207.2 8.6 %collective-permute-done.25 = bf16[1,128,512]{2,1,0:T(8,128)(2,1)S(1)} collective-permute-done((bf16[1,128,512]{2,1,0:T(8,128)(2,1)S(1)}, bf16[1,128,512]{2,1,0:T(8,128)(2,1)S(1)}, u32[]{:S(2)}, u32[]{:S(2)}) %collective-permute-start.25) | collective-permute-done | bytes 131104 | tf_op jit(solution)/shard_map/ppermute | solution.py:48
  217.5 10.0 %while.43 = (s32[]{:T(128)}, bf16[4,128,512]{2,1,0:T(8,128)(2,1)}, pred[4,4]{1,0:T(4,128)(4,1)S(1)}, bf16[4,4,128,128]{3,2,1,0:T(8,128)(2,1)}, s32[4,4]{1,0:T(4,...) while((s32[]{:T(128)}, bf16[4,128,512]{2,1,0:T(8,128)(2,1)}, pred[4,4]{1,0:T(4,128)(4,1)S(1)}, ...), condition=%wide.region_13.16_spmd, body=%wide.region_12.15_spmd.sunk | while | flops 67437592 | bytes 1971369 | solution.py:65
  218.2 1.9 fusion.86
  223.2 1.9 fusion.86
  225.7 1.9 fusion.86
  230.9 28.9 %all_to_all.12 = bf16[4,1,512,512]{3,2,1,0:T(8,128)(2,1)S(1)} all-to-all(bf16[4,1,512,512]{3,2,1,0:T(8,128)(2,1)S(1)} %maximum_bitcast_fusion), channel_id=1, replica_groups=mesh['segment'=4,'dom'=8] {'segment'}, dimensions={0} | all-to-all | bytes 4194304 | tf_op jit(solution)/shard_map/all_to_all | solution.py:109
  (246 shorter events, 62.8 us)
Async XLA Ops:
  6.5 1.6 copy-start
  6.5 60.9 %all-gather.5.cloned.1.call-start = ((), (), s32[]{:S(2)}) async-start(), calls=%async_computation.1 | async-start | bytes 2621440 | tf_op jit(solution)/shard_map/all_gather | solution.py:86
  7.3 77.0 %all-gather.7.cloned.1.call-start = ((), (), s32[]{:S(2)}) async-start(), calls=%async_computation.2 | async-start | bytes 2621440 | tf_op jit(solution)/shard_map/all_gather | solution.py:87
  14.7 1.7 copy-start.14
  17.3 8.4 %copy-start.19 = (bf16[1,512]{1,0:T(2,128)(2,1)S(1)}, bf16[1,512]{1,0:T(2,128)(2,1)}, u32[]{:S(2)}) copy-start(bf16[1,512]{1,0:T(2,128)(2,1)} %param.30) | copy-start | bytes 3076
  17.4 28.6 %collective-permute-start = (bf16[1,128,512]{2,1,0:T(8,128)(2,1)S(1)}, bf16[1,128,512]{2,1,0:T(8,128)(2,1)}, u32[]{:S(2)}, u32[]{:S(2)}) collective-permute-start(bf16[1,128,512]{2,1,0:T(8,128)(2,1)S(1)} %get-tuple-element.222), channel_id=1, source_target_pairs={{0,1},{1,0},{2,3},{3,2},{4,5},{5,4},{6,7},{7,6},{8,9},{9,8},{10,11... | collective-permute-start | bytes 393224 | tf_op jit(solution)/shard_map/ppermute | solution.py:48
  17.9 32.6 %collective-permute-start.1 = (bf16[1,128,512]{2,1,0:T(8,128)(2,1)S(1)}, bf16[1,128,512]{2,1,0:T(8,128)(2,1)}, u32[]{:S(2)}, u32[]{:S(2)}) collective-permute-start(bf16[1,128,512]{2,1,0:T(8,128)(2,1)S(1)} %get-tuple-element.221), channel_id=1, source_target_pairs={{0,2},{1,3},{2,0},{3,1},{4,6},{5,7},{6,4},{7,5},{8,10},{9,11},{10,... | collective-permute-start | bytes 393224 | tf_op jit(solution)/shard_map/ppermute | solution.py:48
  20.6 31.0 %collective-permute-start.2 = (bf16[1,128,512]{2,1,0:T(8,128)(2,1)S(1)}, bf16[1,128,512]{2,1,0:T(8,128)(2,1)}, u32[]{:S(2)}, u32[]{:S(2)}) collective-permute-start(bf16[1,128,512]{2,1,0:T(8,128)(2,1)S(1)} %get-tuple-element.220), channel_id=1, source_target_pairs={{0,3},{1,2},{2,1},{3,0},{4,7},{5,6},{6,5},{7,4},{8,11},{9,10},{10,... | collective-permute-start | bytes 393224 | tf_op jit(solution)/shard_map/ppermute | solution.py:48
  20.6 31.9 %collective-permute-start.3 = (bf16[1,128,512]{2,1,0:T(8,128)(2,1)S(1)}, bf16[1,128,512]{2,1,0:T(8,128)(2,1)}, u32[]{:S(2)}, u32[]{:S(2)}) collective-permute-start(bf16[1,128,512]{2,1,0:T(8,128)(2,1)S(1)} %get-tuple-element.219), channel_id=1, source_target_pairs={{0,4},{1,5},{2,6},{3,7},{4,0},{5,1},{6,2},{7,3},{8,12},{9,13},{10,... | collective-permute-start | bytes 393224 | tf_op jit(solution)/shard_map/ppermute | solution.py:48
  23.4 30.0 %collective-permute-start.4 = (bf16[1,128,512]{2,1,0:T(8,128)(2,1)S(1)}, bf16[1,128,512]{2,1,0:T(8,128)(2,1)}, u32[]{:S(2)}, u32[]{:S(2)}) collective-permute-start(bf16[1,128,512]{2,1,0:T(8,128)(2,1)S(1)} %get-tuple-element.218), channel_id=1, source_target_pairs={{0,5},{1,4},{2,7},{3,6},{4,1},{5,0},{6,3},{7,2},{8,13},{9,12},{10,... | collective-permute-start | bytes 393224 | tf_op jit(solution)/shard_map/ppermute | solution.py:48
  24.4 34.1 %copy-start.16 = (s32[1024]{0:T(1024)}, s32[1024]{0:T(1024)S(1)}, u32[]{:S(2)}) copy-start(s32[1024]{0:T(1024)S(1)} %pad_clamp_fusion.4) | copy-start | bytes 12292
  46.0 8.3 %collective-permute-start.5 = (bf16[1,128,512]{2,1,0:T(8,128)(2,1)S(1)}, bf16[1,128,512]{2,1,0:T(8,128)(2,1)S(1)}, u32[]{:S(2)}, u32[]{:S(2)}) collective-permute-start(bf16[1,128,512]{2,1,0:T(8,128)(2,1)S(1)} %get-tuple-element.217), channel_id=1, source_target_pairs={{0,6},{1,7},{2,4},{3,5},{4,2},{5,3},{6,0},{7,1},{8,14},{9,15},{10,... | collective-permute-start | bytes 393224 | tf_op jit(solution)/shard_map/ppermute | solution.py:48
  50.5 6.4 %collective-permute-start.6 = (bf16[1,128,512]{2,1,0:T(8,128)(2,1)S(1)}, bf16[1,128,512]{2,1,0:T(8,128)(2,1)S(1)}, u32[]{:S(2)}, u32[]{:S(2)}) collective-permute-start(bf16[1,128,512]{2,1,0:T(8,128)(2,1)S(1)} %get-tuple-element.216), channel_id=1, source_target_pairs={{0,7},{1,6},{2,5},{3,4},{4,3},{5,2},{6,1},{7,0},{8,15},{9,14},{10,... | collective-permute-start | bytes 393224 | tf_op jit(solution)/shard_map/ppermute | solution.py:48
  58.5 1.4 copy-start.20
  84.2 2.2 copy-start.12
  84.2 2.2 copy-start.13
  91.6 8.0 %collective-permute-start.7 = (bf16[1,128,512]{2,1,0:T(8,128)(2,1)S(1)}, bf16[1,128,512]{2,1,0:T(8,128)(2,1)S(1)}, u32[]{:S(2)}, u32[]{:S(2)}) collective-permute-start(bf16[1,128,512]{2,1,0:T(8,128)(2,1)S(1)} %get-tuple-element.215), channel_id=1, source_target_pairs={{0,1},{1,0},{2,3},{3,2},{4,5},{5,4},{6,7},{7,6},{8,9},{9,8},{10,11... | collective-permute-start | bytes 393224 | tf_op jit(solution)/shard_map/ppermute | solution.py:48
  95.2 11.3 %collective-permute-start.8 = (bf16[1,128,512]{2,1,0:T(8,128)(2,1)S(1)}, bf16[1,128,512]{2,1,0:T(8,128)(2,1)S(1)}, u32[]{:S(2)}, u32[]{:S(2)}) collective-permute-start(bf16[1,128,512]{2,1,0:T(8,128)(2,1)S(1)} %get-tuple-element.214), channel_id=1, source_target_pairs={{0,2},{1,3},{2,0},{3,1},{4,6},{5,7},{6,4},{7,5},{8,10},{9,11},{10,... | collective-permute-start | bytes 393224 | tf_op jit(solution)/shard_map/ppermute | solution.py:48
  96.7 11.7 %collective-permute-start.9 = (bf16[1,128,512]{2,1,0:T(8,128)(2,1)S(1)}, bf16[1,128,512]{2,1,0:T(8,128)(2,1)S(1)}, u32[]{:S(2)}, u32[]{:S(2)}) collective-permute-start(bf16[1,128,512]{2,1,0:T(8,128)(2,1)S(1)} %get-tuple-element.213), channel_id=1, source_target_pairs={{0,3},{1,2},{2,1},{3,0},{4,7},{5,6},{6,5},{7,4},{8,11},{9,10},{10,... | collective-permute-start | bytes 393224 | tf_op jit(solution)/shard_map/ppermute | solution.py:48
  97.1 11.4 %collective-permute-start.10 = (bf16[1,128,512]{2,1,0:T(8,128)(2,1)S(1)}, bf16[1,128,512]{2,1,0:T(8,128)(2,1)S(1)}, u32[]{:S(2)}, u32[]{:S(2)}) collective-permute-start(bf16[1,128,512]{2,1,0:T(8,128)(2,1)S(1)} %get-tuple-element.212), channel_id=1, source_target_pairs={{0,4},{1,5},{2,6},{3,7},{4,0},{5,1},{6,2},{7,3},{8,12},{9,13},{10,... | collective-permute-start | bytes 393224 | tf_op jit(solution)/shard_map/ppermute | solution.py:48
  99.5 17.9 %collective-permute-start.11 = (bf16[1,128,512]{2,1,0:T(8,128)(2,1)S(1)}, bf16[1,128,512]{2,1,0:T(8,128)(2,1)S(1)}, u32[]{:S(2)}, u32[]{:S(2)}) collective-permute-start(bf16[1,128,512]{2,1,0:T(8,128)(2,1)S(1)} %get-tuple-element.211), channel_id=1, source_target_pairs={{0,5},{1,4},{2,7},{3,6},{4,1},{5,0},{6,3},{7,2},{8,13},{9,12},{10,... | collective-permute-start | bytes 393224 | tf_op jit(solution)/shard_map/ppermute | solution.py:48
  99.7 17.8 %collective-permute-start.12 = (bf16[1,128,512]{2,1,0:T(8,128)(2,1)S(1)}, bf16[1,128,512]{2,1,0:T(8,128)(2,1)S(1)}, u32[]{:S(2)}, u32[]{:S(2)}) collective-permute-start(bf16[1,128,512]{2,1,0:T(8,128)(2,1)S(1)} %get-tuple-element.210), channel_id=1, source_target_pairs={{0,6},{1,7},{2,4},{3,5},{4,2},{5,3},{6,0},{7,1},{8,14},{9,15},{10,... | collective-permute-start | bytes 393224 | tf_op jit(solution)/shard_map/ppermute | solution.py:48
  106.6 10.9 %collective-permute-start.13 = (bf16[1,128,512]{2,1,0:T(8,128)(2,1)S(1)}, bf16[1,128,512]{2,1,0:T(8,128)(2,1)S(1)}, u32[]{:S(2)}, u32[]{:S(2)}) collective-permute-start(bf16[1,128,512]{2,1,0:T(8,128)(2,1)S(1)} %get-tuple-element.209), channel_id=1, source_target_pairs={{0,7},{1,6},{2,5},{3,4},{4,3},{5,2},{6,1},{7,0},{8,15},{9,14},{10,... | collective-permute-start | bytes 393224 | tf_op jit(solution)/shard_map/ppermute | solution.py:48
  119.2 10.0 %copy-start.4 = (f32[512,512]{1,0:T(8,128)S(1)}, f32[512,512]{1,0:T(8,128)}, u32[]{:S(2)}) copy-start(f32[512,512]{1,0:T(8,128)} %fusion.47) | copy-start | bytes 3145732
  129.3 2.0 copy-start.10
  129.3 2.0 copy-start.11
  136.0 13.5 %collective-permute-start.14 = (bf16[1,128,512]{2,1,0:T(8,128)(2,1)S(1)}, bf16[1,128,512]{2,1,0:T(8,128)(2,1)S(1)}, u32[]{:S(2)}, u32[]{:S(2)}) collective-permute-start(bf16[1,128,512]{2,1,0:T(8,128)(2,1)S(1)} %get-tuple-element.208), channel_id=1, source_target_pairs={{0,1},{1,0},{2,3},{3,2},{4,5},{5,4},{6,7},{7,6},{8,9},{9,8},{10,11... | collective-permute-start | bytes 393224 | tf_op jit(solution)/shard_map/ppermute | solution.py:48
  140.2 11.6 %collective-permute-start.15 = (bf16[1,128,512]{2,1,0:T(8,128)(2,1)S(1)}, bf16[1,128,512]{2,1,0:T(8,128)(2,1)S(1)}, u32[]{:S(2)}, u32[]{:S(2)}) collective-permute-start(bf16[1,128,512]{2,1,0:T(8,128)(2,1)S(1)} %get-tuple-element.207), channel_id=1, source_target_pairs={{0,2},{1,3},{2,0},{3,1},{4,6},{5,7},{6,4},{7,5},{8,10},{9,11},{10,... | collective-permute-start | bytes 393224 | tf_op jit(solution)/shard_map/ppermute | solution.py:48
  146.1 11.6 %collective-permute-start.16 = (bf16[1,128,512]{2,1,0:T(8,128)(2,1)S(1)}, bf16[1,128,512]{2,1,0:T(8,128)(2,1)S(1)}, u32[]{:S(2)}, u32[]{:S(2)}) collective-permute-start(bf16[1,128,512]{2,1,0:T(8,128)(2,1)S(1)} %get-tuple-element.206), channel_id=1, source_target_pairs={{0,3},{1,2},{2,1},{3,0},{4,7},{5,6},{6,5},{7,4},{8,11},{9,10},{10,... | collective-permute-start | bytes 393224 | tf_op jit(solution)/shard_map/ppermute | solution.py:48
  146.2 11.5 %collective-permute-start.17 = (bf16[1,128,512]{2,1,0:T(8,128)(2,1)S(1)}, bf16[1,128,512]{2,1,0:T(8,128)(2,1)S(1)}, u32[]{:S(2)}, u32[]{:S(2)}) collective-permute-start(bf16[1,128,512]{2,1,0:T(8,128)(2,1)S(1)} %get-tuple-element.205), channel_id=1, source_target_pairs={{0,4},{1,5},{2,6},{3,7},{4,0},{5,1},{6,2},{7,3},{8,12},{9,13},{10,... | collective-permute-start | bytes 393224 | tf_op jit(solution)/shard_map/ppermute | solution.py:48
  149.2 18.3 %collective-permute-start.18 = (bf16[1,128,512]{2,1,0:T(8,128)(2,1)S(1)}, bf16[1,128,512]{2,1,0:T(8,128)(2,1)S(1)}, u32[]{:S(2)}, u32[]{:S(2)}) collective-permute-start(bf16[1,128,512]{2,1,0:T(8,128)(2,1)S(1)} %get-tuple-element.204), channel_id=1, source_target_pairs={{0,5},{1,4},{2,7},{3,6},{4,1},{5,0},{6,3},{7,2},{8,13},{9,12},{10,... | collective-permute-start | bytes 393224 | tf_op jit(solution)/shard_map/ppermute | solution.py:48
  149.6 17.9 %collective-permute-start.19 = (bf16[1,128,512]{2,1,0:T(8,128)(2,1)S(1)}, bf16[1,128,512]{2,1,0:T(8,128)(2,1)S(1)}, u32[]{:S(2)}, u32[]{:S(2)}) collective-permute-start(bf16[1,128,512]{2,1,0:T(8,128)(2,1)S(1)} %get-tuple-element.203), channel_id=1, source_target_pairs={{0,6},{1,7},{2,4},{3,5},{4,2},{5,3},{6,0},{7,1},{8,14},{9,15},{10,... | collective-permute-start | bytes 393224 | tf_op jit(solution)/shard_map/ppermute | solution.py:48
  151.7 15.7 %collective-permute-start.20 = (bf16[1,128,512]{2,1,0:T(8,128)(2,1)S(1)}, bf16[1,128,512]{2,1,0:T(8,128)(2,1)S(1)}, u32[]{:S(2)}, u32[]{:S(2)}) collective-permute-start(bf16[1,128,512]{2,1,0:T(8,128)(2,1)S(1)} %get-tuple-element.202), channel_id=1, source_target_pairs={{0,7},{1,6},{2,5},{3,4},{4,3},{5,2},{6,1},{7,0},{8,15},{9,14},{10,... | collective-permute-start | bytes 393224 | tf_op jit(solution)/shard_map/ppermute | solution.py:48
  169.3 10.0 %copy-start.5 = (f32[512,512]{1,0:T(8,128)S(1)}, f32[512,512]{1,0:T(8,128)}, u32[]{:S(2)}) copy-start(f32[512,512]{1,0:T(8,128)} %fusion.46) | copy-start | bytes 3145732
  179.3 2.0 copy-start.9
  186.1 12.2 %collective-permute-start.21 = (bf16[1,128,512]{2,1,0:T(8,128)(2,1)S(1)}, bf16[1,128,512]{2,1,0:T(8,128)(2,1)S(1)}, u32[]{:S(2)}, u32[]{:S(2)}) collective-permute-start(bf16[1,128,512]{2,1,0:T(8,128)(2,1)S(1)} %get-tuple-element.201), channel_id=1, source_target_pairs={{0,1},{1,0},{2,3},{3,2},{4,5},{5,4},{6,7},{7,6},{8,9},{9,8},{10,11... | collective-permute-start | bytes 393224 | tf_op jit(solution)/shard_map/ppermute | solution.py:48
  189.8 14.7 %collective-permute-start.22 = (bf16[1,128,512]{2,1,0:T(8,128)(2,1)S(1)}, bf16[1,128,512]{2,1,0:T(8,128)(2,1)S(1)}, u32[]{:S(2)}, u32[]{:S(2)}) collective-permute-start(bf16[1,128,512]{2,1,0:T(8,128)(2,1)S(1)} %get-tuple-element.200), channel_id=1, source_target_pairs={{0,2},{1,3},{2,0},{3,1},{4,6},{5,7},{6,4},{7,5},{8,10},{9,11},{10,... | collective-permute-start | bytes 393224 | tf_op jit(solution)/shard_map/ppermute | solution.py:48
  195.9 11.2 %collective-permute-start.23 = (bf16[1,128,512]{2,1,0:T(8,128)(2,1)S(1)}, bf16[1,128,512]{2,1,0:T(8,128)(2,1)S(1)}, u32[]{:S(2)}, u32[]{:S(2)}) collective-permute-start(bf16[1,128,512]{2,1,0:T(8,128)(2,1)S(1)} %get-tuple-element.199), channel_id=1, source_target_pairs={{0,3},{1,2},{2,1},{3,0},{4,7},{5,6},{6,5},{7,4},{8,11},{9,10},{10,... | collective-permute-start | bytes 393224 | tf_op jit(solution)/shard_map/ppermute | solution.py:48
  195.9 11.2 %collective-permute-start.24 = (bf16[1,128,512]{2,1,0:T(8,128)(2,1)S(1)}, bf16[1,128,512]{2,1,0:T(8,128)(2,1)S(1)}, u32[]{:S(2)}, u32[]{:S(2)}) collective-permute-start(bf16[1,128,512]{2,1,0:T(8,128)(2,1)S(1)} %get-tuple-element.198), channel_id=1, source_target_pairs={{0,4},{1,5},{2,6},{3,7},{4,0},{5,1},{6,2},{7,3},{8,12},{9,13},{10,... | collective-permute-start | bytes 393224 | tf_op jit(solution)/shard_map/ppermute | solution.py:48
  197.8 17.9 %collective-permute-start.25 = (bf16[1,128,512]{2,1,0:T(8,128)(2,1)S(1)}, bf16[1,128,512]{2,1,0:T(8,128)(2,1)S(1)}, u32[]{:S(2)}, u32[]{:S(2)}) collective-permute-start(bf16[1,128,512]{2,1,0:T(8,128)(2,1)S(1)} %get-tuple-element.197), channel_id=1, source_target_pairs={{0,5},{1,4},{2,7},{3,6},{4,1},{5,0},{6,3},{7,2},{8,13},{9,12},{10,... | collective-permute-start | bytes 393224 | tf_op jit(solution)/shard_map/ppermute | solution.py:48
  198.3 17.5 %collective-permute-start.26 = (bf16[1,128,512]{2,1,0:T(8,128)(2,1)S(1)}, bf16[1,128,512]{2,1,0:T(8,128)(2,1)S(1)}, u32[]{:S(2)}, u32[]{:S(2)}) collective-permute-start(bf16[1,128,512]{2,1,0:T(8,128)(2,1)S(1)} %get-tuple-element.196), channel_id=1, source_target_pairs={{0,6},{1,7},{2,4},{3,5},{4,2},{5,3},{6,0},{7,1},{8,14},{9,15},{10,... | collective-permute-start | bytes 393224 | tf_op jit(solution)/shard_map/ppermute | solution.py:48
  204.5 11.3 %collective-permute-start.27 = (bf16[1,128,512]{2,1,0:T(8,128)(2,1)S(1)}, bf16[1,128,512]{2,1,0:T(8,128)(2,1)S(1)}, u32[]{:S(2)}, u32[]{:S(2)}) collective-permute-start(bf16[1,128,512]{2,1,0:T(8,128)(2,1)S(1)} %get-tuple-element.195), channel_id=1, source_target_pairs={{0,7},{1,6},{2,5},{3,4},{4,3},{5,2},{6,1},{7,0},{8,15},{9,14},{10,... | collective-permute-start | bytes 393224 | tf_op jit(solution)/shard_map/ppermute | solution.py:48
  217.5 10.0 %copy-start.3 = (f32[512,512]{1,0:T(8,128)S(1)}, f32[512,512]{1,0:T(8,128)}, u32[]{:S(2)}) copy-start(f32[512,512]{1,0:T(8,128)} %fusion.45) | copy-start | bytes 3145732
  227.5 2.0 copy-start.17
  227.5 2.0 copy-start.18
  229.3 1.2 copy-start.7
  229.3 1.3 copy-start.8
  259.8 2.3 copy-start.1
  (3 other events, 2.7 us)
Sparse Core Ops, SparseCore 0:
  9.2 37.9 all-gather.4
  49.0 35.1 all-gather.6
